TPU v7x, 32 devices: a whole 2x2x4 slice. The times are simulated.
32 devices in a mesh: pat: 8 (over z, core), pb: 4 (over y, x).
Axes of the slice: x: 2, y: 2, z: 4, core: 2. Of those that a mesh axis runs over, the one named last changes fastest.
Arguments:
- measured: float32 [16384, 4096], P(('pat', 'pb')), may hold values from 1 to 10
- resolution: float32 [33, 4096], replicated, may hold values from 0.05 to 1
- loadings_start: float32 [16384, 128], P('pat'), may hold values from 0.05 to 0.5
- components_start: float32 [128, 4096], P(None, 'pb'), may hold values from 0.05 to 0.5
Outputs:
- loadings: float32 [16384, 128], P('pat')
- components: float32 [128, 4096], P(None, 'pb')
All inputs are finite; a program needn't handle non-finite values.
Results may differ from a plain program's by a relative error of at most 0.00013.
Values sent between devices are 32-bit elements; how exact they have to be, the bound alone decides.
A program may use at most 384 MiB of HBM per device.

v0:
```python
import jax
import jax.numpy as jnp
from jax import lax
from jax.sharding import PartitionSpec as P

RADIUS = 16
ITERS = 3


def smear_forward(field, resolution):
    width = field.shape[1]
    padded = jnp.pad(field, ((0, 0), (RADIUS, RADIUS)))
    total = jnp.zeros(field.shape, jnp.float32)
    for offset in range(2 * RADIUS + 1):
        total = total + resolution[offset][None, :] * padded[:, offset : offset + width]
    return total


def smear_back(field, resolution):
    width = field.shape[1]
    total = jnp.zeros(field.shape, jnp.float32)
    for offset in range(2 * RADIUS + 1):
        weighted = jnp.pad(resolution[offset][None, :] * field, ((0, 0), (RADIUS, RADIUS)))
        begin = 2 * RADIUS - offset
        total = total + weighted[:, begin : begin + width]
    return total


def local(measured, resolution, loadings_start, components_start):
    high = lax.Precision.HIGHEST
    blurred = smear_forward(measured, resolution)
    back = smear_back(measured / blurred, resolution)
    weight_sum = smear_back(jnp.ones((1, measured.shape[1]), jnp.float32), resolution)
    corrected_rows = measured * back / weight_sum
    corrected = lax.all_to_all(corrected_rows, "pb", split_axis=1, concat_axis=0, tiled=True)
    loadings = loadings_start
    components = components_start
    for step in range(ITERS):
        quotient = corrected / jnp.dot(loadings, components, precision=high)
        numerator = jnp.dot(loadings.T, quotient, precision=high)
        w_totals = jnp.sum(loadings, axis=0)
        share_num, share_tot = (
            lax.psum_scatter(numerator, "pat", scatter_dimension=0, tiled=True),
            lax.psum_scatter(w_totals, "pat", scatter_dimension=0, tiled=True),
        )
        share_rows = share_num.shape[0]
        first_comp = lax.axis_index("pat") * share_rows
        own_rows = lax.dynamic_slice_in_dim(components, first_comp, share_rows, 0)
        components = lax.all_gather(
            own_rows * share_num / share_tot[:, None], "pat", axis=0, tiled=True
        )
        quotient = corrected / jnp.dot(loadings, components, precision=high)
        w_numer = jnp.dot(quotient, components.T, precision=high)
        share_load = lax.psum_scatter(w_numer, "pb", scatter_dimension=0, tiled=True)
        own_count = share_load.shape[0]
        h_totals = lax.psum(jnp.sum(components, axis=1), "pb")
        first_pat = lax.axis_index("pb") * own_count
        own_load = lax.dynamic_slice_in_dim(loadings, first_pat, own_count, 0)
        loadings = lax.all_gather(
            own_load * share_load / h_totals[None, :], "pb", axis=0, tiled=True
        )
    return (loadings, components)


def solution(mesh):
    return jax.shard_map(
        local,
        mesh=mesh,
        in_specs=(P(("pat", "pb"), None), P(), P("pat", None), P(None, "pb")),
        out_specs=(P("pat", None), P(None, "pb")),
        check_vma=False,
    )
```

profile of v0, /device:TPU:0, one launch (start us, length us, event | category | flops | bytes accessed | tf_op | source)
XLA Modules:
  0.0 877.9 jit_solution(4983352895152377107)
XLA Ops:
  11.9 9.0 %copy.40 = f32[512,4096]{0,1:T(8,128)} copy(f32[512,4096]{1,0:T(8,128)} %param.4) | data formatting | bytes 16777216 | tf_op args[0]
  20.9 146.2 %broadcast_multiply_fusion.31 = (f32[512,4096]{0,1:T(8,128)}, f32[512,4096]{0,1:T(8,128)}) fusion(f32[4096]{0:T(1024)S(1)} %bitcast.137, f32[512,4096]{0,1:T(8,128)} %copy.40, f32[4096]{0:T(1024)S(1)} %bitcast.97, f32[4096]{0:T(1024)S(1)} %bitcast.133, f32[4096]{0:T(1024)S(1)} %bitcast.101, f32[4096]{0:T(1024)S(1)} %bitcast.103, f32[4096]{0:T(1024)S(1)} %bitcast.105, ...), kind=kLoop, calls=%fused_computation.136 | loop fusion | flops 140509184 | bytes 25706496 | tf_op jit(solution)/shard_map/mul | solution.py:23
  167.1 50.9 %broadcast_multiply_fusion.30 = (f32[512,4096]{0,1:T(8,128)}, f32[512,4096]{0,1:T(8,128)}, f32[512,4096]{0,1:T(8,128)}, f32[512,4096]{0,1:T(8,128)}, f32[512,409...) fusion(f32[512,4096]{0,1:T(8,128)} %get-tuple-element.9, ...), kind=kLoop, calls=%fused_computation.135 | loop fusion | flops 37748736 | bytes 159678464 | tf_op jit(solution)/shard_map/mul | solution.py:23
  218.0 34.4 %broadcast_multiply_fusion.29 = (f32[512,4096]{0,1:T(8,128)}, f32[512,4096]{0,1:T(8,128)}, f32[512,4096]{0,1:T(8,128)}, f32[512,4096]{0,1:T(8,128)}, f32[512,409...) fusion(f32[512,4096]{0,1:T(8,128)S(1)} %copy-done, ...), kind=kLoop, calls=%fused_computation.134 | loop fusion | flops 27262976 | bytes 117653504 | tf_op jit(solution)/shard_map/mul | solution.py:23
  254.5 86.5 %fusion.33 = f32[512,4096]{0,1:T(8,128)} fusion(f32[512,4096]{0,1:T(8,128)} %copy.40, f32[512,4096]{0,1:T(8,128)} %get-tuple-element.17, f32[512,4096]{0,1:T(8,128)} %get-tuple-element.16, f32[512,4096]{0,1:T(8,128)} %get-tuple-element.15, f32[512,4096]{0,1:T(8,128)} %get-tuple-element.14, f32[512,4096]{0,1:T(8,128)} %get-tuple-element.13, ...), kind=kLoop, calls=%fused_computation.65 | loop fusion | flops 73400320 | bytes 293634048 | tf_op jit(solution)/shard_map/div | solution.py:34
  347.4 8.8 %fusion.99 = f32[2048,1024]{1,0:T(8,128)} fusion(f32[2048,128]{1,0:T(8,128)S(1)} %copy-done.3, f32[128,1024]{1,0:T(8,128)S(1)} %copy-done.4), kind=kOutput, calls=%fused_computation.210 | convolution fusion | flops 3221225472 | bytes 9961472 | tf_op jit(solution)/shard_map/dot_general | solution.py:39
  356.3 84.4 %all-to-all-done = f32[512,4,1024]{0,2,1:T(8,128)} async-done(((f32[512,4,1024]{0,2,1:T(8,128)}), f32[512,4,1024]{0,2,1:T(8,128)}, u32[]{:S(2)}, u32[]{:S(2)}) %all-to-all-start) | async-done | bytes 8388640 | tf_op jit(solution)/shard_map/all_to_all | solution.py:35
  440.7 8.7 copy.41
  449.4 16.8 %fusion.62 = f32[128,1024]{0,1:T(8,128)S(1)} fusion(f32[2048,128]{1,0:T(8,128)S(1)} %copy-done.3, f32[2048,1024]{1,0:T(8,128)} %bitcast.65, f32[2048,1024]{1,0:T(8,128)} %fusion.99), kind=kOutput, calls=%fused_computation.137 | convolution fusion | flops 3223322624 | bytes 18350080 | tf_op jit(solution)/shard_map/dot_general | solution.py:40
  468.9 16.2 %all-reduce.65 = f32[128]{0:T(128)S(1)} all-reduce(f32[128]{0:T(128)S(1)} %reduce_sum.54), channel_id=3, replica_groups=mesh['pat'=8,'pb'=4] {'pat'}, use_global_device_ids=true, to_apply=%region_2.3.clone | all-reduce | flops 128 | bytes 1024
  485.1 9.1 %copy.43 = f32[2048,1024]{0,1:T(8,128)} copy(f32[2048,1024]{1,0:T(8,128)} %bitcast.66) | data formatting | bytes 16777216 | tf_op jit(solution)/shard_map/all_to_all | solution.py:35
  500.5 15.2 %all_gather.18 = f32[128,1024]{1,0:T(8,128)S(1)} all-gather(f32[16,1024]{1,0:T(8,128)S(1)} %multiply_divide_fusion.5), channel_id=1, replica_groups=mesh['pat'=8,'pb'=4] {'pat'}, dimensions={0}, use_global_device_ids=true | all-gather | bytes 589824 | tf_op jit(solution)/shard_map/all_gather | solution.py:49
  522.8 14.5 %fusion.51 = f32[2048,128]{1,0:T(8,128)} fusion(f32[128,1024]{1,0:T(8,128)S(1)} %all_gather.18, f32[2048,1024]{0,1:T(8,128)S(1)} %bitcast.72, f32[1024,2048]{1,0:T(8,128)S(1)} %fusion.100), kind=kOutput, calls=%fused_computation.94 | convolution fusion | flops 3223322624 | bytes 18350080 | tf_op jit(solution)/shard_map/dot_general | solution.py:53
  537.5 10.0 %psum.21 = f32[128]{0:T(128)S(1)} all-reduce(f32[128]{0:T(128)S(1)} %reduce_sum.55), channel_id=1, replica_groups=mesh['pat'=8,'pb'=4] {'pb'}, use_global_device_ids=true, to_apply=%region_5.6 | all-reduce | flops 128 | bytes 1024 | tf_op jit(solution)/shard_map/psum | solution.py:56
  547.6 16.0 %reduce-scatter.13.cloned.1.call-done = f32[512,128]{1,0:T(8,128)} async-done(((f32[2048,128]{1,0:T(8,128)}), f32[512,128]{1,0:T(8,128)}) %reduce-scatter.13.cloned.1.call-update) | async-done | bytes 262160 | tf_op jit(solution)/shard_map/reduce_scatter | solution.py:54
  565.7 26.8 %all-gather.4.cloned.1.call-done = f32[2048,128]{1,0:T(8,128)} async-done(((f32[512,128]{1,0:T(8,128)}), f32[2048,128]{1,0:T(8,128)}) %all-gather.4.cloned.1.call-update) | async-done | bytes 1048592 | tf_op jit(solution)/shard_map/all_gather | solution.py:59
  600.9 9.7 %fusion.58 = f32[128,1024]{1,0:T(8,128)} fusion(f32[2048,128]{1,0:T(8,128)S(1)} %copy-done.2, f32[2048,1024]{1,0:T(8,128)} %bitcast.67, f32[2048,1024]{1,0:T(8,128)S(1)} %fusion.101), kind=kOutput, calls=%fused_computation.101 | convolution fusion | flops 3223322624 | bytes 18350080
  611.1 16.3 %all-reduce.66 = f32[128]{0:T(128)S(1)} all-reduce(f32[128]{0:T(128)S(1)} %reduce_sum.56), channel_id=6, replica_groups=mesh['pat'=8,'pb'=4] {'pat'}, use_global_device_ids=true, to_apply=%region_8.9.clone | all-reduce | flops 128 | bytes 1024
  627.4 14.7 %reduce-scatter.21.cloned.1.call-done = f32[16,1024]{1,0:T(8,128)} async-done(((f32[128,1024]{1,0:T(8,128)}), f32[16,1024]{1,0:T(8,128)}) %reduce-scatter.21.cloned.1.call-update) | async-done | bytes 65552 | tf_op jit(solution)/shard_map/reduce_scatter | solution.py:43
  643.1 14.9 %all_gather.20 = f32[128,1024]{1,0:T(8,128)S(1)} all-gather(f32[16,1024]{1,0:T(8,128)S(1)} %multiply_divide_fusion.4), channel_id=1, replica_groups=mesh['pat'=8,'pb'=4] {'pat'}, dimensions={0}, use_global_device_ids=true | all-gather | bytes 589824 | tf_op jit(solution)/shard_map/all_gather | solution.py:49
  665.0 9.9 %fusion.56 = f32[2048,128]{1,0:T(8,128)} fusion(f32[128,1024]{1,0:T(8,128)S(1)} %all_gather.20, f32[2048,1024]{1,0:T(8,128)} %bitcast.68, f32[2048,1024]{1,0:T(8,128)S(1)} %fusion.102), kind=kOutput, calls=%fused_computation.99 | convolution fusion | flops 3223322624 | bytes 18350080 | tf_op jit(solution)/shard_map/dot_general | solution.py:53
  675.1 10.1 %psum.22 = f32[128]{0:T(128)S(1)} all-reduce(f32[128]{0:T(128)S(1)} %reduce_sum.57), channel_id=1, replica_groups=mesh['pat'=8,'pb'=4] {'pb'}, use_global_device_ids=true, to_apply=%region_11.12 | all-reduce | flops 128 | bytes 1024 | tf_op jit(solution)/shard_map/psum | solution.py:56
  685.2 16.1 %reduce-scatter.15.cloned.1.call-done = f32[512,128]{1,0:T(8,128)} async-done(((f32[2048,128]{1,0:T(8,128)}), f32[512,128]{1,0:T(8,128)}) %reduce-scatter.15.cloned.1.call-update) | async-done | bytes 262160 | tf_op jit(solution)/shard_map/reduce_scatter | solution.py:54
  703.3 26.8 %all-gather.6.cloned.1.call-done = f32[2048,128]{1,0:T(8,128)} async-done(((f32[512,128]{1,0:T(8,128)}), f32[2048,128]{1,0:T(8,128)}) %all-gather.6.cloned.1.call-update) | async-done | bytes 1048592 | tf_op jit(solution)/shard_map/all_gather | solution.py:59
  738.5 9.7 %fusion.54 = f32[128,1024]{1,0:T(8,128)} fusion(f32[2048,128]{1,0:T(8,128)S(1)} %copy-done.1, f32[2048,1024]{1,0:T(8,128)} %bitcast.69, f32[2048,1024]{1,0:T(8,128)S(1)} %fusion.103), kind=kOutput, calls=%fused_computation.97 | convolution fusion | flops 3223322624 | bytes 18350080
  748.8 16.2 %all-reduce.67 = f32[128]{0:T(128)S(1)} all-reduce(f32[128]{0:T(128)S(1)} %reduce_sum.58), channel_id=9, replica_groups=mesh['pat'=8,'pb'=4] {'pat'}, use_global_device_ids=true, to_apply=%region_14.15.clone | all-reduce | flops 128 | bytes 1024
  765.0 14.8 %reduce-scatter.23.cloned.1.call-done = f32[16,1024]{1,0:T(8,128)} async-done(((f32[128,1024]{1,0:T(8,128)}), f32[16,1024]{1,0:T(8,128)}) %reduce-scatter.23.cloned.1.call-update) | async-done | bytes 65552 | tf_op jit(solution)/shard_map/reduce_scatter | solution.py:43
  780.8 14.9 %all_gather.22 = f32[128,1024]{1,0:T(8,128)S(1)} all-gather(f32[16,1024]{1,0:T(8,128)S(1)} %multiply_divide_fusion.3), channel_id=1, replica_groups=mesh['pat'=8,'pb'=4] {'pat'}, dimensions={0}, use_global_device_ids=true | all-gather | bytes 589824 | tf_op jit(solution)/shard_map/all_gather | solution.py:49
  802.7 9.9 %fusion.52 = f32[2048,128]{1,0:T(8,128)} fusion(f32[128,1024]{1,0:T(8,128)S(1)} %all_gather.22, f32[2048,1024]{1,0:T(8,128)} %bitcast.70, f32[2048,1024]{1,0:T(8,128)S(1)} %fusion.104), kind=kOutput, calls=%fused_computation.95 | convolution fusion | flops 3223322624 | bytes 18350080 | tf_op jit(solution)/shard_map/dot_general | solution.py:53
  812.8 10.1 %psum.23 = f32[128]{0:T(128)S(1)} all-reduce(f32[128]{0:T(128)S(1)} %reduce_sum.59), channel_id=1, replica_groups=mesh['pat'=8,'pb'=4] {'pb'}, use_global_device_ids=true, to_apply=%region_17.18 | all-reduce | flops 128 | bytes 1024 | tf_op jit(solution)/shard_map/psum | solution.py:56
  822.8 16.1 %reduce-scatter.17.cloned.1.call-done = f32[512,128]{1,0:T(8,128)} async-done(((f32[2048,128]{1,0:T(8,128)}), f32[512,128]{1,0:T(8,128)}) %reduce-scatter.17.cloned.1.call-update) | async-done | bytes 262160 | tf_op jit(solution)/shard_map/reduce_scatter | solution.py:54
  840.6 27.3 %all-gather.8.cloned.1.call-done = f32[2048,128]{1,0:T(8,128)} async-done(((f32[512,128]{1,0:T(8,128)}), f32[2048,128]{1,0:T(8,128)}) %all-gather.8.cloned.1.call-update) | async-done | bytes 1048592 | tf_op jit(solution)/shard_map/all_gather | solution.py:59
  (64 shorter events, 71.4 us)
Async XLA Ops:
  167.1 50.9 %copy-start = (f32[512,4096]{0,1:T(8,128)S(1)}, f32[512,4096]{0,1:T(8,128)}, u32[]{:S(2)}) copy-start(f32[512,4096]{0,1:T(8,128)} %get-tuple-element.9) | copy-start | bytes 25165828
  341.0 6.4 copy-start.3
  341.0 6.4 copy-start.4
  341.0 99.7 %all-to-all-start = ((f32[512,4,1024]{0,2,1:T(8,128)}), f32[512,4,1024]{0,2,1:T(8,128)}, u32[]{:S(2)}, u32[]{:S(2)}) async-start(f32[512,4,1024]{0,2,1:T(8,128)} %bitcast.64), calls=%async_computation | async-start | bytes 16777216 | tf_op jit(solution)/shard_map/all_to_all | solution.py:35
  346.9 152.6 %reduce-scatter.19.cloned.1.call-start = ((), (), s32[]{:S(2)}) async-start(), calls=%async_computation.13 | async-start | bytes 589824 | tf_op jit(solution)/shard_map/reduce_scatter | solution.py:43
  449.4 18.2 %copy-start.5 = (u32[32]{0:T(128)S(1)}, u32[32]{0:T(128)}, u32[]{:S(2)}) copy-start(u32[32]{0:T(128)} %constant.154) | copy-start | bytes 388
  467.3 96.2 %reduce-scatter.13.cloned.1.call-start = ((), (), s32[]{:S(2)}) async-start(), calls=%async_computation.7 | async-start | bytes 1310720 | tf_op jit(solution)/shard_map/reduce_scatter | solution.py:54
  499.4 23.4 %slice-start = ((s8[8388608]{0:T(1024)(128)(4,1)}), s8[4194304]{0:T(1024)(128)(4,1)S(1)}, s32[]{:S(2)}) async-start(s8[8388608]{0:T(1024)(128)(4,1)} %bitcast.71), calls=%async_computation.16 | async-start | bytes 8388608
  515.7 7.1 slice-start.1
  537.4 55.1 %all-gather.4.cloned.1.call-start = ((), (), s32[]{:S(2)}) async-start(), calls=%async_computation.8 | async-start | bytes 1310720 | tf_op jit(solution)/shard_map/all_gather | solution.py:59
  565.3 76.9 %reduce-scatter.21.cloned.1.call-start = ((), (), s32[]{:S(2)}) async-start(), calls=%async_computation.14 | async-start | bytes 589824 | tf_op jit(solution)/shard_map/reduce_scatter | solution.py:43
  592.5 8.3 copy-start.2
  610.7 90.6 %reduce-scatter.15.cloned.1.call-start = ((), (), s32[]{:S(2)}) async-start(), calls=%async_computation.9 | async-start | bytes 1310720 | tf_op jit(solution)/shard_map/reduce_scatter | solution.py:54
  674.9 55.2 %all-gather.6.cloned.1.call-start = ((), (), s32[]{:S(2)}) async-start(), calls=%async_computation.10 | async-start | bytes 1310720 | tf_op jit(solution)/shard_map/all_gather | solution.py:59
  703.0 76.8 %reduce-scatter.23.cloned.1.call-start = ((), (), s32[]{:S(2)}) async-start(), calls=%async_computation.15 | async-start | bytes 589824 | tf_op jit(solution)/shard_map/reduce_scatter | solution.py:43
  730.1 8.3 copy-start.1
  748.4 90.5 %reduce-scatter.17.cloned.1.call-start = ((), (), s32[]{:S(2)}) async-start(), calls=%async_computation.11 | async-start | bytes 1310720 | tf_op jit(solution)/shard_map/reduce_scatter | solution.py:54
  812.6 55.3 %all-gather.8.cloned.1.call-start = ((), (), s32[]{:S(2)}) async-start(), calls=%async_computation.12 | async-start | bytes 1310720 | tf_op jit(solution)/shard_map/all_gather | solution.py:59
Sparse Core Ops, SparseCore 0:
  467.4 31.9 reduce-scatter.18
  537.5 26.0 reduce-scatter.12
  566.0 26.4 all-gather.3
  610.9 31.2 reduce-scatter.20
  675.0 26.2 reduce-scatter.14
  703.6 26.4 all-gather.5
  748.5 31.2 reduce-scatter.22
  812.7 26.1 reduce-scatter.16
  841.3 26.4 all-gather.7
where the time goes:
time: 886 us; the launch traced here: 878 us
  other arithmetic  329 us (37%)
  waiting for transfers between devices  249 us (28%)
  blocking collectives  124 us (14%)
  matrix products  117 us (13%)
  local copies, waits for them, and re-layouts  36.5 us (4%)
  between operations  15.2 us (2%)
    mul x3, other arithmetic, smear_back(): resolution[offset][None, :] * field  232 us
    div x1, other arithmetic, local(): corrected_rows = measured * back / weight_sum  86.5 us
    all_to_all x1, waiting for transfers between devices, local(): lax.all_to_all(corrected_rows, 'pb', split_axis=1, concat_axis=0, tiled=T...  84.4 us
    all_gather x3, waiting for transfers between devices, local(): lax.all_gather(own_load * share_load / h_totals[None, :], 'pb', axis=0, t...  80.9 us
    unnamed x3, blocking collectives  48.6 us
    reduce_scatter x3, waiting for transfers between devices, local(): lax.psum_scatter(w_numer, 'pb', scatter_dimension=0, tiled=True)  48.2 us
    dot_general x6, matrix products, local(): quotient = corrected / jnp.dot(loadings, components, precision=high)  46.4 us
    all_gather x3, blocking collectives, local(): lax.all_gather(own_rows * share_num / share_tot[:, None], 'pat', axis=0,...  45.1 us
  transfers between devices with their start and end apart: 10, of which 10 were waited for; matrix products, arithmetic and copies ran while one was open for 2% of the time, Pallas kernels for 0%

commit v1 on v0

v1 whole, which is shorter than its diff:
```python
import jax
import jax.numpy as jnp
from jax import lax
from jax.experimental import pallas as pl
from jax.experimental.pallas import tpu as pltpu
from jax.sharding import PartitionSpec as P

ITERS = 3
LANES = 128
BAND = 256
AXES = ("pat", "pb")


def split(x):
    high = x.astype(jnp.bfloat16)
    return high, (x - high.astype(jnp.float32)).astype(jnp.bfloat16)


def dot(a, b):
    return jnp.dot(a, b, preferred_element_type=jnp.float32)


def dot_nt(a, b):
    return lax.dot_general(
        a, b, (((1,), (1,)), ((), ())), preferred_element_type=jnp.float32
    )


def smear_kernel(taps, v_ref, r_ref, out_ref, bh, bl, vh, vl, acc, wacc):
    rows, width = v_ref.shape
    blocks = width // BAND
    radius = taps // 2
    window = BAND + 2 * LANES

    @pl.when(pl.program_id(0) == 0)
    def _():
        wacc[...] = jnp.zeros_like(wacc)

        @pl.loop(0, blocks)
        def _(j):
            at = pl.multiple_of(j * BAND, BAND)
            weights = r_ref[pl.ds(at, BAND), :]
            wide = jnp.concatenate(
                [weights, jnp.zeros((BAND, window - LANES), jnp.float32)], axis=1
            )
            band = pltpu.roll(wide, LANES - radius, 1, stride=1, stride_axis=0)
            bh[j], bl[j] = split(band)
            wacc[:, pl.ds(at, window)] += jnp.broadcast_to(
                jnp.sum(band, axis=0, keepdims=True), (8, window)
            )

    edge = jnp.zeros((rows, LANES), jnp.bfloat16)
    for ref in (vh, vl):
        ref[:, :LANES] = edge
        ref[:, width + LANES :] = edge

    @pl.loop(0, blocks)
    def _(j):
        at = pl.multiple_of(j * BAND, BAND)
        high, low = split(v_ref[:, pl.ds(at, BAND)])
        vh[:, pl.ds(at + LANES, BAND)] = high
        vl[:, pl.ds(at + LANES, BAND)] = low
        acc[:, pl.ds(at, BAND)] = jnp.zeros((rows, BAND), jnp.float32)

    acc[:, width:] = jnp.zeros((rows, 2 * LANES), jnp.float32)

    @pl.loop(0, blocks)
    def _(j):
        at = pl.multiple_of(j * BAND, BAND)
        kh, kl = bh[j], bl[j]
        xh = vh[:, pl.ds(at, window)]
        blurred = dot_nt(xh, kh) + dot_nt(xh, kl) + dot_nt(vl[:, pl.ds(at, window)], kh)
        uh, ul = split(v_ref[:, pl.ds(at, BAND)] / blurred)
        acc[:, pl.ds(at, window)] += dot(uh, kh) + dot(uh, kl) + dot(ul, kh)

    @pl.loop(0, blocks)
    def _(j):
        at = pl.multiple_of(j * BAND, BAND)
        here = pl.ds(at + LANES, BAND)
        out_ref[:, pl.ds(at, BAND)] = (
            v_ref[:, pl.ds(at, BAND)] * acc[:, here] / wacc[:1, here]
        )


def correct(measured, resolution):
    total, width = measured.shape
    taps = resolution.shape[0]
    rows = min(total, 256)
    weights = jnp.pad(resolution.T, ((0, 0), (0, LANES - taps)))
    blocks = width // BAND
    window = BAND + 2 * LANES
    padded = width + 2 * LANES

    def body(*refs):
        smear_kernel(taps, *refs)

    return pl.pallas_call(
        body,
        grid=(total // rows,),
        out_shape=jax.ShapeDtypeStruct(measured.shape, jnp.float32),
        in_specs=[
            pl.BlockSpec((rows, width), lambda i: (i, 0)),
            pl.BlockSpec((width, LANES), lambda i: (0, 0)),
        ],
        out_specs=pl.BlockSpec((rows, width), lambda i: (i, 0)),
        scratch_shapes=[
            pltpu.VMEM((blocks, BAND, window), jnp.bfloat16),
            pltpu.VMEM((blocks, BAND, window), jnp.bfloat16),
            pltpu.VMEM((rows, padded), jnp.bfloat16),
            pltpu.VMEM((rows, padded), jnp.bfloat16),
            pltpu.VMEM((rows, padded), jnp.float32),
            pltpu.VMEM((8, padded), jnp.float32),
        ],
        cost_estimate=pl.CostEstimate(
            flops=12 * total * width * window, bytes_accessed=8 * total * width,
            transcendentals=0,
        ),
        name="smear",
    )(measured, weights)


def quotient_of(x_ref, l, c_ref):
    c = jnp.concatenate([c_ref[i] for i in range(c_ref.shape[0])], axis=1)
    lh, ll = split(l)
    ch, cl = split(c)
    model = dot(
        jnp.concatenate([lh, ll, lh], axis=1), jnp.concatenate([ch, ch, cl], axis=0)
    )
    qh, ql = split(x_ref[...] / model)
    return qh, ql, ch, cl


def numer_kernel(x_ref, l_ref, lt_ref, c_ref, out_ref):
    comps = l_ref.shape[1]
    l = l_ref[...]
    qh, ql, _, _ = quotient_of(x_ref, l, c_ref)
    th, tl = split(lt_ref[...])
    both = dot(jnp.concatenate([th, tl], axis=0), qh)
    numer = both[:comps] + both[comps:] + dot(th, ql)
    totals = jnp.broadcast_to(jnp.sum(l, axis=0, keepdims=True), (8, comps))
    for i in range(c_ref.shape[0]):
        out_ref[i, :comps, :] = numer[:, i * LANES : (i + 1) * LANES]
        out_ref[i, comps:, :] = totals


def load_kernel(x_ref, l_ref, c_ref, l_out, lt_out, acc, sums):
    comps = l_ref.shape[1]
    step = pl.program_id(0)

    @pl.when(step == 0)
    def _():
        acc[...] = jnp.zeros_like(acc)
        sums[...] = jnp.zeros_like(sums)

    l = l_ref[...]
    qh, ql, ch, cl = quotient_of(x_ref, l, c_ref)
    both = dot_nt(qh, jnp.concatenate([ch, cl], axis=0))
    acc[...] += both[:, :comps] + both[:, comps:] + dot_nt(ql, ch)
    here = c_ref[0]
    for i in range(1, c_ref.shape[0]):
        here = here + c_ref[i]
    sums[...] += here

    @pl.when(step == pl.num_programs(0) - 1)
    def _():
        totals = jnp.sum(sums[...].T, axis=0, keepdims=True)
        new = l * acc[...] / totals
        l_out[...] = new
        lt_out[...] = new.T


def cost(x, comps):
    return pl.CostEstimate(
        flops=12 * x.size * comps, bytes_accessed=4 * x.size, transcendentals=0
    )


STEP = 512


def numerators(x, l, lt, c):
    rows, width = x.shape
    comps = l.shape[1]
    per = STEP // LANES
    return pl.pallas_call(
        numer_kernel,
        grid=(width // STEP,),
        out_shape=jax.ShapeDtypeStruct((width // LANES, comps + 8, LANES), jnp.float32),
        in_specs=[
            pl.BlockSpec((rows, STEP), lambda i: (0, i)),
            pl.BlockSpec((rows, comps), lambda i: (0, 0)),
            pl.BlockSpec((comps, rows), lambda i: (0, 0)),
            pl.BlockSpec((per, comps, LANES), lambda i: (i, 0, 0)),
        ],
        out_specs=pl.BlockSpec((per, comps + 8, LANES), lambda i: (i, 0, 0)),
        cost_estimate=cost(x, comps),
        name="numer",
    )(x, l, lt, c)


def new_loadings(x, l, c):
    rows, width = x.shape
    comps = l.shape[1]
    per = STEP // LANES
    return pl.pallas_call(
        load_kernel,
        grid=(width // STEP,),
        out_shape=(
            jax.ShapeDtypeStruct((rows, comps), jnp.float32),
            jax.ShapeDtypeStruct((comps, rows), jnp.float32),
        ),
        in_specs=[
            pl.BlockSpec((rows, STEP), lambda i: (0, i)),
            pl.BlockSpec((rows, comps), lambda i: (0, 0)),
            pl.BlockSpec((per, comps, LANES), lambda i: (i, 0, 0)),
        ],
        out_specs=(
            pl.BlockSpec((rows, comps), lambda i: (0, 0)),
            pl.BlockSpec((comps, rows), lambda i: (0, 0)),
        ),
        scratch_shapes=[
            pltpu.VMEM((rows, comps), jnp.float32),
            pltpu.VMEM((comps, LANES), jnp.float32),
        ],
        cost_estimate=cost(x, comps),
        name="loads",
    )(x, l, c)


def regroup(blocks, count):
    if blocks.shape[0] == count:
        return blocks
    comps = blocks.shape[1]
    flat = jnp.swapaxes(blocks, 0, 1).reshape(comps, -1)
    return jnp.swapaxes(flat.reshape(comps, count, -1), 0, 1)


def scatter(num):
    blocks, height, cols = num.shape
    flat = num.reshape(blocks * height, cols)
    flat = lax.psum_scatter(flat, "pat", scatter_dimension=0, tiled=True)
    flat = lax.psum_scatter(flat, "pb", scatter_dimension=0, tiled=True)
    return flat.reshape(1, height, cols)


def local(devices, measured, resolution, loadings_start, components_start):
    rows, width = measured.shape
    comps = loadings_start.shape[1]
    cols = width // devices
    lane_blocks = width // LANES
    first_row = lax.axis_index("pb") * rows
    l = lax.dynamic_slice_in_dim(loadings_start, first_row, rows, 0)
    lt = l.T
    start = regroup(components_start[None], components_start.shape[1] // LANES)
    c = lax.all_gather(start, "pb", axis=0, tiled=True)
    own = lax.dynamic_slice_in_dim(
        regroup(c, devices), lax.axis_index(AXES), 1, 0
    )
    x = correct(measured, resolution)
    for step in range(ITERS):
        num = numerators(x, l, lt, c)
        if cols != LANES:
            extra = -(-comps // cols)
            totals = jnp.pad(num[0, comps], (0, extra * cols - comps))
            totals = jnp.broadcast_to(
                totals.reshape(1, extra, cols), (devices, extra, cols)
            )
            num = jnp.concatenate([regroup(num[:, :comps], devices), totals], axis=1)
        share = scatter(num)
        totals = share[0, comps:].reshape(-1)[:comps]
        own = own * share[:, :comps] / totals[None, :, None]
        c = regroup(lax.all_gather(own, AXES, axis=0, tiled=True), lane_blocks)
        l, lt = new_loadings(x, l, c)
    loadings = lax.all_gather(l, "pb", axis=0, tiled=True)
    count = components_start.shape[1] // LANES
    mine = lax.dynamic_slice_in_dim(c, lax.axis_index("pb") * count, count, 0)
    return loadings, jnp.swapaxes(mine, 0, 1).reshape(comps, -1)


def solution(mesh):
    devices = mesh.shape["pat"] * mesh.shape["pb"]

    def body(*args):
        return local(devices, *args)

    return jax.shard_map(
        body,
        mesh=mesh,
        in_specs=(P(("pat", "pb"), None), P(), P("pat", None), P(None, "pb")),
        out_specs=(P("pat", None), P(None, "pb")),
        check_vma=False,
    )
```

time: 886 us -> 520 us (0.59)
  other arithmetic: 329 us -> 4.68 us
  waiting for transfers between devices: 249 us -> 380 us
  blocking collectives: 124 us -> 0 us
  matrix products: 117 us -> 0 us
  Pallas kernels: 0 us -> 106 us
  local copies, waits for them, and re-layouts: 36.5 us -> 13.7 us
    mul x3 -> x0, other arithmetic: 232 us -> none  [smear_back(): resolution[offset][None, :] * field]
    all_gather x3 -> x5, waiting for transfers between devices: 80.9 us -> 194 us  [the longest x3 171 us: local(): c = regroup(lax.all_gather(own, AXES, axis=0, tiled=True), lane_blocks)]
    pallas_call x0 -> x7, Pallas kernels: none -> 106 us  [the longest x1 44.2 us: correct(): pl.pallas_call(body, grid=(total // rows,), out_shape=jax.ShapeDtypeStruc...]
    dot_general x10 -> x0, matrix products: 97.6 us -> none  [the longest x6 46.4 us: local(): quotient = corrected / jnp.dot(loadings, components, precision=high)]
    div x7 -> x3, other arithmetic: 94.5 us -> 4.68 us  [local(): own = own * share[:, :comps] / totals[None, :, None]]
    all_to_all x1 -> x0, waiting for transfers between devices: 84.4 us -> none  [local(): lax.all_to_all(corrected_rows, 'pb', split_axis=1, concat_axis=0, tiled=T...]
    unnamed x9 -> x14, waiting for transfers between devices: 0.57 us -> 75.2 us
    unnamed x3 -> x0, blocking collectives: 48.6 us -> none
  transfers between devices with their start and end apart: 10 -> 11, of which waited for: 10 -> 10; matrix products, arithmetic and copies ran while one was open for 2% -> 1% of each run, Pallas kernels for 0% -> 9%
where the time goes in v1:
time: 520 us; the launch traced here: 518 us
  waiting for transfers between devices  380 us (73%)
  Pallas kernels  106 us (20%)
  between operations  14 us (3%)
  local copies, waits for them, and re-layouts  13.7 us (3%)
    all_gather x3, waiting for transfers between devices, local(): c = regroup(lax.all_gather(own, AXES, axis=0, tiled=True), lane_blocks)  171 us
    reduce_scatter x3, waiting for transfers between devices, scatter(): flat = lax.psum_scatter(flat, 'pat', scatter_dimension=0, tiled=True)  111 us
    unnamed x14, waiting for transfers between devices  75.2 us
    pallas_call x1, Pallas kernels, correct(): pl.pallas_call(body, grid=(total // rows,), out_shape=jax.ShapeDtypeStruc...  44.2 us
    pallas_call x3, Pallas kernels, numerators(): pl.pallas_call(numer_kernel, grid=(width // STEP,), out_shape=jax.ShapeDt...  31 us
    pallas_call x3, Pallas kernels, new_loadings(): pl.pallas_call(load_kernel, grid=(width // STEP,), out_shape=(jax.ShapeDt...  30.8 us
    all_gather x1, waiting for transfers between devices, local(): loadings = lax.all_gather(l, 'pb', axis=0, tiled=True)  23.2 us
  transfers between devices with their start and end apart: 11, of which 10 were waited for; matrix products, arithmetic and copies ran while one was open for 1% of the time, Pallas kernels for 9%

profile of v1, /device:TPU:0, one launch (start us, length us, event | category | flops | bytes accessed | tf_op | source)
XLA Modules:
  0.0 518.4 jit_solution(10413368987056406178)
XLA Ops:
  7.2 1.3 copy.15
  8.5 1.0 copy.16
  9.7 0.9 copy.17.lt_ref
  10.5 1.7 copy.14
  12.3 1.5 pad.4.refs_1_
  13.8 0.7 constant_dynamic-slice_fusion.1.l_ref
  14.5 44.2 %smear.1.x_ref = f32[512,4096]{1,0:T(8,128)} custom-call(f32[512,4096]{1,0:T(8,128)} %refs_0_.1, f32[4096,128]{1,0:T(8,128)} %pad.4.refs_1_), custom_call_target="tpu_custom_call" | custom-call | flops 12884901888 | bytes 16777216 | tf_op jit(solution)/shard_map/smear/pallas_call | solution.py:97
  58.7 10.3 %numer.3 = f32[32,136,128]{2,1,0:T(8,128)} custom-call(f32[512,4096]{1,0:T(8,128)} %smear.1.x_ref, f32[512,128]{1,0:T(8,128)} %constant_dynamic-slice_fusion.1.l_ref, f32[128,512]{1,0:T(8,128)} %copy.17.lt_ref, f32[32,128,128]{2,1,0:T(8,128)} %all-gather.6.cloned.1.call-done.c_ref), custom_call_target="tpu_custom_call" | custom-call | flops 3221225472 | bytes 8388608 | tf_op jit(solution)/shard_map/numer/pallas_call | solution.py:185
  69.1 39.5 %reduce-scatter.13.cloned.1.call-done = f32[544,128]{1,0:T(8,128)} async-done(((f32[4352,128]{1,0:T(8,128)}), f32[544,128]{1,0:T(8,128)}) %reduce-scatter.13.cloned.1.call-update) | async-done | bytes 278544 | tf_op jit(solution)/shard_map/reduce_scatter | solution.py:241
  108.7 24.9 %reduce-scatter.19.cloned.1.call-done = f32[136,128]{1,0:T(8,128)} async-done(((f32[544,128]{1,0:T(8,128)}), f32[136,128]{1,0:T(8,128)}) %reduce-scatter.19.cloned.1.call-update) | async-done | bytes 69648
  133.6 0.7 slice_bitcast_fusion.2
  134.2 1.6 fusion.2
  135.9 56.6 %all-gather.8.cloned.1.call-done.c_ref = f32[32,128,128]{2,1,0:T(8,128)} async-done(((f32[1,128,128]{2,1,0:T(8,128)}), f32[32,128,128]{2,1,0:T(8,128)}) %all-gather.8.cloned.1.call-update) | async-done | bytes 2097168 | tf_op jit(solution)/shard_map/all_gather | solution.py:272
  192.5 10.3 %loads.3 = (f32[512,128]{1,0:T(8,128)}, f32[128,512]{1,0:T(8,128)}) custom-call(f32[512,4096]{1,0:T(8,128)} %smear.1.x_ref, f32[512,128]{1,0:T(8,128)} %constant_dynamic-slice_fusion.1.l_ref, f32[32,128,128]{2,1,0:T(8,128)} %all-gather.8.cloned.1.call-done.c_ref), custom_call_target="tpu_custom_call" | custom-call | flops 3221225472 | bytes 8388608 | tf_op jit(solution)/shard_map/loads/pallas_call | solution.py:205
  202.8 10.3 %numer.4 = f32[32,136,128]{2,1,0:T(8,128)} custom-call(f32[512,4096]{1,0:T(8,128)} %smear.1.x_ref, f32[512,128]{1,0:T(8,128)} %get-tuple-element.7.l_ref, f32[128,512]{1,0:T(8,128)} %get-tuple-element.8.lt_ref, f32[32,128,128]{2,1,0:T(8,128)} %all-gather.8.cloned.1.call-done.c_ref), custom_call_target="tpu_custom_call" | custom-call | flops 3221225472 | bytes 8388608 | tf_op jit(solution)/shard_map/numer/pallas_call | solution.py:185
  213.2 35.5 %reduce-scatter.15.cloned.1.call-done = f32[544,128]{1,0:T(8,128)} async-done(((f32[4352,128]{1,0:T(8,128)}), f32[544,128]{1,0:T(8,128)}) %reduce-scatter.15.cloned.1.call-update) | async-done | bytes 278544 | tf_op jit(solution)/shard_map/reduce_scatter | solution.py:241
  248.8 24.8 %reduce-scatter.21.cloned.1.call-done = f32[136,128]{1,0:T(8,128)} async-done(((f32[544,128]{1,0:T(8,128)}), f32[136,128]{1,0:T(8,128)}) %reduce-scatter.21.cloned.1.call-update) | async-done | bytes 69648
  273.6 0.7 slice_bitcast_fusion.1
  274.3 1.5 fusion.1
  275.9 56.8 %all-gather.10.cloned.1.call-done.c_ref = f32[32,128,128]{2,1,0:T(8,128)} async-done(((f32[1,128,128]{2,1,0:T(8,128)}), f32[32,128,128]{2,1,0:T(8,128)}) %all-gather.10.cloned.1.call-update) | async-done | bytes 2097168 | tf_op jit(solution)/shard_map/all_gather | solution.py:272
  332.8 10.3 %loads.4 = (f32[512,128]{1,0:T(8,128)}, f32[128,512]{1,0:T(8,128)}) custom-call(f32[512,4096]{1,0:T(8,128)} %smear.1.x_ref, f32[512,128]{1,0:T(8,128)} %get-tuple-element.7.l_ref, f32[32,128,128]{2,1,0:T(8,128)} %all-gather.10.cloned.1.call-done.c_ref), custom_call_target="tpu_custom_call" | custom-call | flops 3221225472 | bytes 8388608 | tf_op jit(solution)/shard_map/loads/pallas_call | solution.py:205
  343.0 10.3 %numer.5 = f32[32,136,128]{2,1,0:T(8,128)} custom-call(f32[512,4096]{1,0:T(8,128)} %smear.1.x_ref, f32[512,128]{1,0:T(8,128)} %get-tuple-element.9.l_ref, f32[128,512]{1,0:T(8,128)} %get-tuple-element.10.lt_ref, f32[32,128,128]{2,1,0:T(8,128)} %all-gather.10.cloned.1.call-done.c_ref), custom_call_target="tpu_custom_call" | custom-call | flops 3221225472 | bytes 8388608 | tf_op jit(solution)/shard_map/numer/pallas_call | solution.py:185
  353.4 35.5 %reduce-scatter.17.cloned.1.call-done = f32[544,128]{1,0:T(8,128)} async-done(((f32[4352,128]{1,0:T(8,128)}), f32[544,128]{1,0:T(8,128)}) %reduce-scatter.17.cloned.1.call-update) | async-done | bytes 278544 | tf_op jit(solution)/shard_map/reduce_scatter | solution.py:241
  389.0 25.3 %reduce-scatter.23.cloned.1.call-done = f32[136,128]{1,0:T(8,128)} async-done(((f32[544,128]{1,0:T(8,128)}), f32[136,128]{1,0:T(8,128)}) %reduce-scatter.23.cloned.1.call-update) | async-done | bytes 69648
  414.3 0.7 slice_bitcast_fusion
  415.0 1.6 fusion
  416.6 57.2 %all-gather.12.cloned.1.call-done.c_ref = f32[32,128,128]{2,1,0:T(8,128)} async-done(((f32[1,128,128]{2,1,0:T(8,128)}), f32[32,128,128]{2,1,0:T(8,128)}) %all-gather.12.cloned.1.call-update) | async-done | bytes 2097168 | tf_op jit(solution)/shard_map/all_gather | solution.py:272
  473.8 10.2 %loads.5 = (f32[512,128]{1,0:T(8,128)}, f32[128,512]{1,0:T(8,128)}) custom-call(f32[512,4096]{1,0:T(8,128)} %smear.1.x_ref, f32[512,128]{1,0:T(8,128)} %get-tuple-element.9.l_ref, f32[32,128,128]{2,1,0:T(8,128)} %all-gather.12.cloned.1.call-done.c_ref), custom_call_target="tpu_custom_call" | custom-call | flops 3221225472 | bytes 8388608 | tf_op jit(solution)/shard_map/loads/pallas_call | solution.py:205
  484.1 1.1 constant_dynamic-slice_fusion
  485.4 1.0 copy.19
  486.4 23.2 %all-gather.14.cloned.1.call-done = f32[2048,128]{1,0:T(8,128)} async-done(((f32[512,128]{1,0:T(8,128)}), f32[2048,128]{1,0:T(8,128)}) %all-gather.14.cloned.1.call-update) | async-done | bytes 1048592 | tf_op jit(solution)/shard_map/all_gather | solution.py:274
  509.6 2.3 copy.22
  (31 shorter events, 0.9 us)
Async XLA Ops:
  7.2 2.5 copy-start
  7.2 51.5 %all-gather.6.cloned.1.call-start = ((), (), s32[]{:S(2)}) async-start(), calls=%async_computation.6 | async-start | bytes 2621440 | tf_op jit(solution)/shard_map/all_gather | solution.py:255
  9.6 99.0 %reduce-scatter.13.cloned.1.call-start = ((), (), s32[]{:S(2)}) async-start(), calls=%async_computation.7 | async-start | bytes 2506752 | tf_op jit(solution)/shard_map/reduce_scatter | solution.py:241
  69.0 64.5 %reduce-scatter.19.cloned.1.call-start = ((), (), s32[]{:S(2)}) async-start(), calls=%async_computation.14 | async-start | bytes 348160
  108.6 83.9 %all-gather.8.cloned.1.call-start = ((), (), s32[]{:S(2)}) async-start(), calls=%async_computation.8 | async-start | bytes 2162688 | tf_op jit(solution)/shard_map/all_gather | solution.py:272
  135.8 112.9 %reduce-scatter.15.cloned.1.call-start = ((), (), s32[]{:S(2)}) async-start(), calls=%async_computation.9 | async-start | bytes 2506752 | tf_op jit(solution)/shard_map/reduce_scatter | solution.py:241
  213.1 61.2 %copy-start.1 = (f32[1,128,128]{2,1,0:T(8,128)S(1)}, f32[1,128,128]{2,1,0:T(8,128)}, u32[]{:S(2)}) copy-start(f32[1,128,128]{2,1,0:T(8,128)} %fusion.2) | copy-start | bytes 196612
  213.1 60.5 %reduce-scatter.21.cloned.1.call-start = ((), (), s32[]{:S(2)}) async-start(), calls=%async_computation.15 | async-start | bytes 348160
  248.7 84.0 %all-gather.10.cloned.1.call-start = ((), (), s32[]{:S(2)}) async-start(), calls=%async_computation.10 | async-start | bytes 2162688 | tf_op jit(solution)/shard_map/all_gather | solution.py:272
  275.9 113.0 %reduce-scatter.17.cloned.1.call-start = ((), (), s32[]{:S(2)}) async-start(), calls=%async_computation.11 | async-start | bytes 2506752 | tf_op jit(solution)/shard_map/reduce_scatter | solution.py:241
  353.3 61.6 %copy-start.2 = (f32[1,128,128]{2,1,0:T(8,128)S(1)}, f32[1,128,128]{2,1,0:T(8,128)}, u32[]{:S(2)}) copy-start(f32[1,128,128]{2,1,0:T(8,128)} %fusion.1) | copy-start | bytes 196612
  353.4 60.9 %reduce-scatter.23.cloned.1.call-start = ((), (), s32[]{:S(2)}) async-start(), calls=%async_computation.16 | async-start | bytes 348160
  388.9 84.9 %all-gather.12.cloned.1.call-start = ((), (), s32[]{:S(2)}) async-start(), calls=%async_computation.12 | async-start | bytes 2162688 | tf_op jit(solution)/shard_map/all_gather | solution.py:272
  416.5 93.1 %all-gather.14.cloned.1.call-start = ((), (), s32[]{:S(2)}) async-start(), calls=%async_computation.13 | async-start | bytes 1310720 | tf_op jit(solution)/shard_map/all_gather | solution.py:274
Sparse Core Ops, SparseCore 0:
  10.4 37.9 all-gather.5
  69.1 39.4 reduce-scatter.12
  111.5 22.0 reduce-scatter.18
  136.3 56.1 all-gather.7
  213.3 35.4 reduce-scatter.14
  251.4 22.1 reduce-scatter.20
  276.5 56.2 all-gather.9
  353.5 35.3 reduce-scatter.16
  391.8 22.4 reduce-scatter.22
  417.6 56.2 all-gather.11
  484.2 25.3 all-gather.13

commit v2 on v1

--- a/solution.py
+++ b/solution.py
@@ -243,9 +243,140 @@
     return flat.reshape(1, height, cols)
 
 
-def local(devices, measured, resolution, loadings_start, components_start):
+MESH = pl.DeviceIdType.MESH
+
+
+def bits_of(pat, pb):
+    count = pat.bit_length() - 1, pb.bit_length() - 1
+    return (
+        [("pat", 0)]
+        + [("pb", i) for i in range(count[1])]
+        + [("pat", i) for i in range(1, count[0])]
+    )
+
+
+def orders_of(bits):
+    ahead = list(range(len(bits)))
+    other = list(ahead)
+    other[1], other[2] = 2, 1
+    return ahead, other
+
+
+def my_bit(bit):
+    return lax.rem(lax.axis_index(bit[0]) // (1 << bit[1]), 2)
+
+
+def exchange_kernel(bits, groups, comps, num_ref, own_ref, c_ref, new_ref, *scratch):
+    dims = len(bits)
+    mine = [my_bit(b) for b in bits]
+    place = {"pat": lax.axis_index("pat"), "pb": lax.axis_index("pb")}
+    peers = []
+    for (axis, i), bit in zip(bits, mine):
+        moved = place[axis] + (1 - 2 * bit) * (1 << i)
+        peers.append(
+            (moved, place["pb"]) if axis == "pat" else (place["pat"], moved)
+        )
+    count = len(groups)
+    bufs = [scratch[g * dims : (g + 1) * dims] for g in range(count)]
+    send, recv = scratch[count * dims :]
+
+    barrier = pltpu.get_barrier_semaphore()
+    for peer in peers:
+        pl.semaphore_signal(barrier, inc=1, device_id=peer, device_id_type=MESH)
+    pl.semaphore_wait(barrier, dims)
+
+    def remote(src, dst, g, phase, k, d):
+        return pltpu.make_async_remote_copy(
+            src_ref=src,
+            dst_ref=dst,
+            send_sem=send.at[g, phase, k],
+            recv_sem=recv.at[g, phase, k],
+            device_id=peers[d],
+            device_id_type=MESH,
+        )
+
+    def pick(g, k, side):
+        order, first, size = groups[g]
+        left = [d for d in range(dims) if d not in order[:k]]
+        index = [slice(None)] * len(left)
+        index[left.index(order[k])] = side
+        if k == 0:
+            return num_ref, tuple(index) + (pl.ds(first, size),)
+        return bufs[g][k - 1], tuple(index)
+
+    flying = [None] * count
+    for k in range(dims + 1):
+        for g in range(count):
+            if k:
+                flying[g].wait()
+                ref, index = pick(g, k - 1, mine[groups[g][0][k - 1]])
+                bufs[g][k - 1][...] += ref[index]
+            if k < dims:
+                d = groups[g][0][k]
+                ref, index = pick(g, k, 1 - mine[d])
+                flying[g] = remote(ref.at[index], bufs[g][k], g, 0, k, d)
+                flying[g].start()
+
+    sums = jnp.concatenate([bufs[g][dims - 1][...] for g in range(count)], axis=0)
+    totals = jnp.broadcast_to(sums[comps : comps + 1], (LANES, comps)).T
+    new = own_ref[...] * sums[:comps] / totals
+    new_ref[...] = new
+    c_ref[tuple(mine)] = new
+
+    for k in range(dims + 1):
+        for g in range(count):
+            order, first, size = groups[g]
+            if k:
+                flying[g].wait()
+            if k < dims:
+                d = order[dims - 1 - k]
+                done = order[dims - k :]
+                index = tuple(slice(None) if e in done else mine[e] for e in range(dims))
+                size = min(size, comps - first)
+                view = c_ref.at[index + (pl.ds(first, size),)]
+                flying[g] = remote(view, view, g, 1, k, d)
+                flying[g].start()
+
+
+def exchange(bits, num, own):
+    blocks, height, cols = num.shape
+    comps = own.shape[0]
+    dims = len(bits)
+    cut = comps // 2
+    groups = [
+        (order, first, size)
+        for order, first, size in zip(orders_of(bits), (0, cut), (cut, height - cut))
+    ]
+    shape = (2,) * dims
+
+    def body(*refs):
+        exchange_kernel(bits, groups, comps, *refs)
+
+    vmem = pl.BlockSpec(memory_space=pltpu.VMEM)
+    c, new = pl.pallas_call(
+        body,
+        out_shape=(
+            jax.ShapeDtypeStruct(shape + (comps, cols), jnp.float32),
+            jax.ShapeDtypeStruct((comps, cols), jnp.float32),
+        ),
+        in_specs=[vmem, vmem],
+        out_specs=(vmem, vmem),
+        scratch_shapes=[
+            pltpu.VMEM((2,) * (dims - 1 - k) + (size, cols), jnp.float32)
+            for _, _, size in groups
+            for k in range(dims)
+        ]
+        + [pltpu.SemaphoreType.DMA((len(groups), 2, dims))] * 2,
+        compiler_params=pltpu.CompilerParams(collective_id=0, has_side_effects=True),
+        name="exchange",
+    )(num.reshape(shape + (height, cols)), own)
+    return c.reshape(blocks, comps, cols), new
+
+
+def local(sizes, measured, resolution, loadings_start, components_start):
     rows, width = measured.shape
     comps = loadings_start.shape[1]
+    devices = sizes[0] * sizes[1]
     cols = width // devices
     lane_blocks = width // LANES
     first_row = lax.axis_index("pb") * rows
@@ -253,12 +384,22 @@
     lt = l.T
     start = regroup(components_start[None], components_start.shape[1] // LANES)
     c = lax.all_gather(start, "pb", axis=0, tiled=True)
-    own = lax.dynamic_slice_in_dim(
-        regroup(c, devices), lax.axis_index(AXES), 1, 0
-    )
+    bits = bits_of(*sizes)
+    paired = cols == LANES == comps and 1 << len(bits) == devices and sizes[1] >= 4
+    position = lax.axis_index(AXES)
+    if paired:
+        position = 0
+        for bit in bits:
+            position = 2 * position + my_bit(bit)
+    own = lax.dynamic_slice_in_dim(regroup(c, devices), position, 1, 0)
     x = correct(measured, resolution)
     for step in range(ITERS):
         num = numerators(x, l, lt, c)
+        if paired:
+            c, new = exchange(bits, num, own[0])
+            own = new[None]
+            l, lt = new_loadings(x, l, c)
+            continue
         if cols != LANES:
             extra = -(-comps // cols)
             totals = jnp.pad(num[0, comps], (0, extra * cols - comps))
@@ -278,10 +419,10 @@
 
 
 def solution(mesh):
-    devices = mesh.shape["pat"] * mesh.shape["pb"]
+    sizes = mesh.shape["pat"], mesh.shape["pb"]
 
     def body(*args):
-        return local(devices, *args)
+        return local(sizes, *args)
 
     return jax.shard_map(
         body,

time: 520 us -> 306 us (0.59)
  waiting for transfers between devices: 380 us -> 24.4 us
  Pallas kernels: 106 us -> 253 us
    all_gather x3 -> x0, waiting for transfers between devices: 171 us -> none  [local(): c = regroup(lax.all_gather(own, AXES, axis=0, tiled=True), lane_blocks)]
    pallas_call x0 -> x3, Pallas kernels: none -> 147 us  [exchange(): pl.pallas_call(body, out_shape=(jax.ShapeDtypeStruct(shape + (comps, cols...]
    reduce_scatter x3 -> x0, waiting for transfers between devices: 111 us -> none  [scatter(): flat = lax.psum_scatter(flat, 'pat', scatter_dimension=0, tiled=True)]
    unnamed x14 -> x2, waiting for transfers between devices: 75.2 us -> 0.03 us
  transfers between devices with their start and end apart: 11 -> 2, of which waited for: 10 -> 1; matrix products, arithmetic and copies ran while one was open for 1% -> 2% of each run, Pallas kernels for 9% -> 14%
where the time goes in v2:
time: 306 us; the launch traced here: 305 us
  Pallas kernels  253 us (83%)
  waiting for transfers between devices  24.4 us (8%)
  between operations  14.2 us (5%)
  local copies, waits for them, and re-layouts  13.2 us (4%)
    pallas_call x3, Pallas kernels, exchange(): pl.pallas_call(body, out_shape=(jax.ShapeDtypeStruct(shape + (comps, cols...  147 us
    pallas_call x1, Pallas kernels, correct(): pl.pallas_call(body, grid=(total // rows,), out_shape=jax.ShapeDtypeStruc...  44.1 us
    pallas_call x3, Pallas kernels, numerators(): pl.pallas_call(numer_kernel, grid=(width // STEP,), out_shape=jax.ShapeDt...  31 us
    pallas_call x3, Pallas kernels, new_loadings(): pl.pallas_call(load_kernel, grid=(width // STEP,), out_shape=(jax.ShapeDt...  30.8 us
    all_gather x1, waiting for transfers between devices, local(): loadings = lax.all_gather(l, 'pb', axis=0, tiled=True)  24.4 us
    unnamed x6, local copies, waits for them, and re-layouts  6.3 us
  transfers between devices with their start and end apart: 2, of which 1 were waited for; matrix products, arithmetic and copies ran while one was open for 2% of the time, Pallas kernels for 14%

profile of v2, /device:TPU:0, one launch (start us, length us, event | category | flops | bytes accessed | tf_op | source)
XLA Modules:
  0.0 305.0 jit_solution(7741220346985473296)
XLA Ops:
  7.2 0.0 copy-start
  7.2 0.0 all-gather.3.cloned.1.call-start
  7.2 1.3 copy.15
  8.5 1.0 copy.16
  9.5 0.0 all-gather.3.cloned.1.call-update
  9.6 0.0 all-gather.5.cloned.1.call-start
  9.7 0.0 copy-done
  9.7 0.9 copy.17.lt_ref
  10.6 1.7 copy.14
  12.3 1.5 pad.4.refs_1_
  13.8 0.7 constant_dynamic-slice_fusion.l_ref
  14.5 44.1 %smear.1.x_ref = f32[512,4096]{1,0:T(8,128)} custom-call(f32[512,4096]{1,0:T(8,128)} %refs_0_.1, f32[4096,128]{1,0:T(8,128)} %pad.4.refs_1_), custom_call_target="tpu_custom_call" | custom-call | flops 12884901888 | bytes 16777216 | tf_op jit(solution)/shard_map/smear/pallas_call | solution.py:97
  58.7 0.0 all-gather.3.cloned.1.call-done.c_ref
  58.7 1.5 dynamic-slice_bitcast_fusion.1.refs_1_
  60.1 10.3 %numer.3 = f32[32,136,128]{2,1,0:T(8,128)} custom-call(f32[512,4096]{1,0:T(8,128)} %smear.1.x_ref, f32[512,128]{1,0:T(8,128)} %constant_dynamic-slice_fusion.l_ref, f32[128,512]{1,0:T(8,128)} %copy.17.lt_ref, f32[32,128,128]{2,1,0:T(8,128)} %all-gather.3.cloned.1.call-done.c_ref), custom_call_target="tpu_custom_call" | custom-call | flops 3221225472 | bytes 8388608 | tf_op jit(solution)/shard_map/numer/pallas_call | solution.py:185
  70.5 50.2 %exchange.3 = (f32[2,2,2,2,2,128,128]{6,5,4,3,2,1,0:T(8,128)}, f32[128,128]{1,0:T(8,128)}) custom-call(f32[2,2,2,2,2,136,128]{6,5,4,3,2,1,0:T(8,128)} %bitcast.19, f32[128,128]{1,0:T(8,128)} %dynamic-slice_bitcast_fusion.1.refs_1_), custom_call_target="tpu_custom_call" | custom-call | tf_op jit(solution)/shard_map/exchange/pallas_call | solution.py:356
  120.6 10.3 %loads.3 = (f32[512,128]{1,0:T(8,128)}, f32[128,512]{1,0:T(8,128)}) custom-call(f32[512,4096]{1,0:T(8,128)} %smear.1.x_ref, f32[512,128]{1,0:T(8,128)} %constant_dynamic-slice_fusion.l_ref, f32[32,128,128]{2,1,0:T(8,128)} %bitcast.21), custom_call_target="tpu_custom_call" | custom-call | flops 3221225472 | bytes 8388608 | tf_op jit(solution)/shard_map/loads/pallas_call | solution.py:205
  130.9 10.3 %numer.4 = f32[32,136,128]{2,1,0:T(8,128)} custom-call(f32[512,4096]{1,0:T(8,128)} %smear.1.x_ref, f32[512,128]{1,0:T(8,128)} %get-tuple-element.13.l_ref, f32[128,512]{1,0:T(8,128)} %get-tuple-element.14.lt_ref, f32[32,128,128]{2,1,0:T(8,128)} %bitcast.22), custom_call_target="tpu_custom_call" | custom-call | flops 3221225472 | bytes 8388608 | tf_op jit(solution)/shard_map/numer/pallas_call | solution.py:185
  141.3 48.8 %exchange.4 = (f32[2,2,2,2,2,128,128]{6,5,4,3,2,1,0:T(8,128)}, f32[128,128]{1,0:T(8,128)}) custom-call(f32[2,2,2,2,2,136,128]{6,5,4,3,2,1,0:T(8,128)} %bitcast.17, f32[128,128]{1,0:T(8,128)} %get-tuple-element.15.refs_1_), custom_call_target="tpu_custom_call" | custom-call | tf_op jit(solution)/shard_map/exchange/pallas_call | solution.py:356
  190.1 10.3 %loads.4 = (f32[512,128]{1,0:T(8,128)}, f32[128,512]{1,0:T(8,128)}) custom-call(f32[512,4096]{1,0:T(8,128)} %smear.1.x_ref, f32[512,128]{1,0:T(8,128)} %get-tuple-element.13.l_ref, f32[32,128,128]{2,1,0:T(8,128)} %bitcast.23), custom_call_target="tpu_custom_call" | custom-call | flops 3221225472 | bytes 8388608 | tf_op jit(solution)/shard_map/loads/pallas_call | solution.py:205
  200.3 10.3 %numer.5 = f32[32,136,128]{2,1,0:T(8,128)} custom-call(f32[512,4096]{1,0:T(8,128)} %smear.1.x_ref, f32[512,128]{1,0:T(8,128)} %get-tuple-element.17.l_ref, f32[128,512]{1,0:T(8,128)} %get-tuple-element.18.lt_ref, f32[32,128,128]{2,1,0:T(8,128)} %bitcast.24), custom_call_target="tpu_custom_call" | custom-call | flops 3221225472 | bytes 8388608 | tf_op jit(solution)/shard_map/numer/pallas_call | solution.py:185
  210.7 48.2 %exchange.5 = (f32[2,2,2,2,2,128,128]{6,5,4,3,2,1,0:T(8,128)}, f32[128,128]{1,0:T(8,128)}) custom-call(f32[2,2,2,2,2,136,128]{6,5,4,3,2,1,0:T(8,128)} %bitcast.18, f32[128,128]{1,0:T(8,128)} %get-tuple-element.19.refs_1_), custom_call_target="tpu_custom_call" | custom-call | tf_op jit(solution)/shard_map/exchange/pallas_call | solution.py:356
  258.9 10.3 %loads.5 = (f32[512,128]{1,0:T(8,128)}, f32[128,512]{1,0:T(8,128)}) custom-call(f32[512,4096]{1,0:T(8,128)} %smear.1.x_ref, f32[512,128]{1,0:T(8,128)} %get-tuple-element.17.l_ref, f32[32,128,128]{2,1,0:T(8,128)} %bitcast.27), custom_call_target="tpu_custom_call" | custom-call | flops 3221225472 | bytes 8388608 | tf_op jit(solution)/shard_map/loads/pallas_call | solution.py:205
  269.1 0.0 all-gather.5.cloned.1.call-update
  269.2 1.1 dynamic-slice_bitcast_fusion
  270.3 0.2 copy.18
  270.5 1.0 copy.19
  271.5 24.4 %all-gather.5.cloned.1.call-done = f32[2048,128]{1,0:T(8,128)} async-done(((f32[512,128]{1,0:T(8,128)}), f32[2048,128]{1,0:T(8,128)}) %all-gather.5.cloned.1.call-update) | async-done | bytes 1048592 | tf_op jit(solution)/shard_map/all_gather | solution.py:415
  295.9 2.3 copy.21
  (1 shorter events, 0.0 us)
Async XLA Ops:
  7.2 2.5 copy-start
  7.2 51.5 %all-gather.3.cloned.1.call-start = ((), (), s32[]{:S(2)}) async-start(), calls=%async_computation | async-start | bytes 2621440 | tf_op jit(solution)/shard_map/all_gather | solution.py:386
  9.6 286.3 %all-gather.5.cloned.1.call-start = ((), (), s32[]{:S(2)}) async-start(), calls=%async_computation.1 | async-start | bytes 1310720 | tf_op jit(solution)/shard_map/all_gather | solution.py:415
Sparse Core Ops, SparseCore 0:
  10.4 37.8 all-gather.2
  269.3 26.5 all-gather.4
